TPU v7x, 512 devices: a whole 4x4x16 slice. The times are simulated.
512 devices in a mesh: fsdp: 32 (over z_lo, y), tp: 16 (over z_hi, x, core).
Axes of the slice: x: 4, y: 4, z: 16 (z_hi: 2, z_lo: 8; z = z_hi * 8 + z_lo), core: 2. Of those that a mesh axis runs over, the one named last changes fastest.
Arguments:
- base_weight: bfloat16 [16384, 26624], P(('fsdp', 'tp')), may hold values from -0.1875 to 0.1875
- left_factor: bfloat16 [16384, 64], P(('fsdp', 'tp')), may hold values from -0.75 to 0.75
- right_factor: bfloat16 [64, 26624], P(None, 'tp'), may hold values from -0.029907227 to 0.029907227
- magnitude: float32 [26624], replicated, may hold values from 6 to 96
Outputs:
- quantized: bfloat16 [16384, 26624], P('fsdp', 'tp')
- block_scales: float32 [128, 208], P('fsdp', 'tp')
All inputs are finite; a program needn't handle non-finite values. Where the computation divides by a largest or mean magnitude, that divisor is 1e-20 or more.
Results may differ from a plain program's by a relative error of at most 0.01.
Values may be sent and summed in bfloat16 or wider, within the bound.
A program may use at most 64 MiB of HBM per device.

v0:
```python
import jax
import jax.numpy as jnp
from jax import lax
from jax.sharding import PartitionSpec as P

BLOCK = 128


epsilon = 1e-06


def to_blocks(merged):
    row_count, col_count = merged.shape
    tile_view = merged.astype(jnp.float32).reshape(
        row_count // BLOCK, BLOCK, col_count // BLOCK, BLOCK
    )
    block_max = jnp.max(jnp.abs(tile_view), axis=(1, 3))
    scaled = tile_view / (block_max[:, None, :, None] + epsilon)
    return (scaled.astype(jnp.bfloat16).reshape(row_count, col_count), block_max)


def body(base_weight, left_factor, right_factor, magnitude):
    combined = base_weight.astype(jnp.float32) + jnp.dot(
        left_factor,
        lax.all_gather(right_factor, "tp", axis=1, tiled=True),
        preferred_element_type=jnp.float32,
    )
    col_squares = lax.psum(jnp.sum(combined * combined, axis=0), ("fsdp", "tp"))
    merged = (magnitude * combined / jnp.sqrt(col_squares + epsilon)).astype(jnp.bfloat16)
    served = lax.all_to_all(merged, "tp", split_axis=1, concat_axis=0, tiled=True)
    quantized, block_scales = to_blocks(served)
    return (quantized, block_scales)


def solution(mesh):
    in_specs = (P(("fsdp", "tp"), None), P(("fsdp", "tp"), None), P(None, "tp"), P())
    out_specs = (P("fsdp", "tp"), P("fsdp", "tp"))
    return jax.shard_map(body, mesh=mesh, in_specs=in_specs, out_specs=out_specs, check_vma=False)
```

profile of v0, /device:TPU:96, one launch (start us, length us, event | category | flops | bytes accessed | tf_op | source)
XLA Modules:
  0.0 683.0 jit_solution(6132133179312654590)
XLA Ops:
  7.2 0.0 copy-start
  7.2 0.0 all-gather.2.cloned.1.call-start
  7.2 0.7 all-gather.2.cloned.1.call-update
  7.9 0.0 copy-start.1
  7.9 0.0 all-reduce.2.cloned.1.call-start
  8.0 114.7 %all-gather.2.cloned.1.call-done = bf16[64,26624]{1,0:T(8,128)(2,1)} async-done(((bf16[64,1664]{1,0:T(8,128)(2,1)}), bf16[64,26624]{1,0:T(8,128)(2,1)}) %all-gather.2.cloned.1.call-update) | async-done | bytes 3407888 | tf_op jit(solution)/shard_map/all_gather | solution.py:25
  122.6 0.0 copy-done
  122.6 4.0 multiply_reduce_fusion
  126.7 0.0 all-reduce.2.cloned.1.call-update
  126.7 445.2 %all-reduce.2.cloned.1.call-done = f32[26624]{0:T(1024)} async-done(((f32[26624]{0:T(1024)}), f32[26624]{0:T(1024)}) %all-reduce.2.cloned.1.call-update) | async-done | bytes 106512 | tf_op jit(solution)/shard_map/psum | solution.py:28
  571.9 0.9 add_sqrt_fusion
  572.8 0.0 copy-done.1
  572.8 0.3 divide_convert_fusion
  573.2 0.1 copy.18
  573.3 91.1 %all_to_all.13 = bf16[32,16,1664]{2,0,1:T(8,128)(2,1)S(1)} all-to-all(bf16[32,16,1664]{2,0,1:T(8,128)(2,1)S(1)} %bitcast.21), channel_id=1, replica_groups=mesh['fsdp'=32,'tp'=16] {'tp'}, dimensions={1} | all-to-all | bytes 3407872 | tf_op jit(solution)/shard_map/all_to_all | solution.py:30
  664.4 0.5 abs_reduce_fusion
  664.9 0.1 reduce_max.18
  665.0 0.0 copy-start.2
  665.0 0.1 copy.11
  665.1 0.5 div.21
  665.6 2.1 copy.17
  667.7 0.0 copy-done.2
  667.7 4.8 copy.12
  672.4 3.7 fusion
  (2 shorter events, 0.0 us)
Async XLA Ops:
  7.2 115.5 %copy-start = (bf16[32,64]{1,0:T(8,128)(2,1)S(1)}, bf16[32,64]{1,0:T(8,128)(2,1)}, u32[]{:S(2)}) copy-start(bf16[32,64]{1,0:T(8,128)(2,1)} %param.5) | copy-start | bytes 12292
  7.2 115.5 %all-gather.2.cloned.1.call-start = ((), (), s32[]{:S(2)}) async-start(), calls=%async_computation.1 | async-start | bytes 3620864 | tf_op jit(solution)/shard_map/all_gather | solution.py:25
  7.9 564.9 %copy-start.1 = (f32[26624]{0:T(1024)S(1)}, f32[26624]{0:T(1024)}, u32[]{:S(2)}) copy-start(f32[26624]{0:T(1024)} %param.7) | copy-start | bytes 319492
  7.9 564.0 %all-reduce.2.cloned.1.call-start = ((), (), s32[]{:S(2)}) async-start(), calls=%async_computation.2 | async-start | bytes 212992 | tf_op jit(solution)/shard_map/psum | solution.py:28
  665.0 2.7 copy-start.2
Sparse Core Ops, SparseCore 0:
  11.3 111.2 all-gather.1
  128.6 443.1 all-reduce.1
where the time goes:
time: 683 us
  waiting for transfers between devices  561 us (82%)
  blocking collectives  91.1 us (13%)
  between operations  14.1 us (2%)
  local copies, waits for them, and re-layouts  7.59 us (1%)
    psum x1, waiting for transfers between devices, body(): col_squares = lax.psum(jnp.sum(combined * combined, axis=0), ('fsdp', 'tp'))  445 us
    all_gather x1, waiting for transfers between devices, body(): lax.all_gather(right_factor, 'tp', axis=1, tiled=True)  115 us
    all_to_all x1, blocking collectives, body(): lax.all_to_all(merged, 'tp', split_axis=1, concat_axis=0, tiled=True)  91.1 us
  transfers between devices with their start and end apart: 2, of which 2 were waited for; matrix products, arithmetic and copies ran while one was open for 0% of the time, Pallas kernels for 0%

commit v1 on v0

v1 whole, which is shorter than its diff:
```python
import functools

import jax
import jax.numpy as jnp
from jax import lax
from jax.experimental import pallas as pl
from jax.experimental.pallas import tpu as pltpu
from jax.sharding import PartitionSpec as P

MESH = pl.DeviceIdType.MESH
BLOCK = 128
EPS = 1e-06
NB = (5, 4, 4)
C0 = (0, 5, 9)
ROWS = 32
COLS = 1664
NX = 4
NY = 4
NZ = 16
HOPS = 8
PLANE = 8


def kernel(w, lf, rf, mag, out, scales, wall, rb, ball, rbb, rfv, magv, comb, outv, *refs):
    psy, psz = refs[:3], refs[3:6]
    scv, ring_s, ring_r, bring_s, bring_r, pl_s, st_r, own_r, bp_s, bp_r, y_s, y_r, z_s, z_r, loc, outs = refs[6:]
    f, t = lax.axis_index("fsdp"), lax.axis_index("tp")
    zlo, y = f // NY, lax.rem(f, NY)
    half, x, core = t // PLANE, lax.rem(t, PLANE) // 2, lax.rem(t, 2)
    z = half * 8 + zlo
    me = x * 2 + core

    def dev(zz, yy, k):
        return (lax.rem(zz, 8) * NY + yy, (zz // 8) * PLANE + k)

    z_up, z_dn = lax.rem(z + 1, NZ), lax.rem(z + NZ - 1, NZ)
    up, dn = dev(z_up, y, me), dev(z_dn, y, me)
    plane = [lax.rem(x + dx, NX) * 2 + lax.rem(core + dc, 2) for dx in (0, 1, 3, 2) for dc in (0, 1)][1:]
    y_peers = [lax.rem(y + d, NY) for d in range(1, NY)]
    z_peers = [lax.rem(zlo + d, 8) for d in range(1, 8)]

    loads = [
        pltpu.make_async_copy(rf, rfv, loc.at[0]),
        pltpu.make_async_copy(mag, magv, loc.at[1]),
        pltpu.make_async_copy(lf, ball.at[pl.ds(pl.multiple_of(t * ROWS, ROWS), ROWS), :], loc.at[2]),
        pltpu.make_async_copy(
            w.at[:, pl.ds(pl.multiple_of(t * COLS, BLOCK), COLS)],
            wall.at[pl.ds(pl.multiple_of(t * ROWS, ROWS), ROWS), :],
            loc.at[3],
        ),
    ]
    far = (1 - half) * PLANE
    own_stage = pltpu.make_async_copy(
        w.at[:, pl.ds(pl.multiple_of((far + me) * COLS, BLOCK), COLS)],
        rb.at[0, pl.ds(pl.multiple_of(me * ROWS, ROWS), ROWS), :],
        loc.at[4],
    )
    own_stage.start()
    for c in loads:
        c.start()

    barrier = pltpu.get_barrier_semaphore()
    peers = [up, dn] + [dev(z, y, k) for k in plane] + [dev(z, q, me) for q in y_peers]
    peers += [dev(half * 8 + q, y, me) for q in z_peers]
    for p in peers:
        pl.semaphore_signal(barrier, inc=1, device_id=p, device_id_type=MESH)
    pl.semaphore_wait(barrier, len(peers))

    def cols(b):
        return pl.ds(C0[b] * BLOCK, NB[b] * BLOCK)

    def stage_copy(b, i):
        k = plane[i]
        return pltpu.make_async_remote_copy(
            w.at[:, pl.ds(pl.multiple_of((far + k) * COLS + C0[b] * BLOCK, BLOCK), NB[b] * BLOCK)],
            rb.at[0, pl.ds(pl.multiple_of(me * ROWS, ROWS), ROWS), cols(b)],
            pl_s.at[0],
            st_r.at[b, me],
            device_id=dev(z, y, k),
            device_id_type=MESH,
        )

    def stage_wait(b, k):
        pltpu.make_async_remote_copy(
            rb.at[0, pl.ds(pl.multiple_of(k * ROWS, ROWS), ROWS), cols(b)],
            rb.at[0, pl.ds(pl.multiple_of(k * ROWS, ROWS), ROWS), cols(b)],
            pl_s.at[0],
            st_r.at[b, k],
            device_id=dev(z, y, k),
            device_id_type=MESH,
        ).wait_recv()

    def own_copy(i):
        k = plane[i]
        return pltpu.make_async_remote_copy(
            w.at[:, pl.ds(pl.multiple_of((half * PLANE + k) * COLS, BLOCK), COLS)],
            wall.at[pl.ds(pl.multiple_of(t * ROWS, ROWS), ROWS), :],
            pl_s.at[0],
            own_r.at[me],
            device_id=dev(z, y, k),
            device_id_type=MESH,
        )

    def own_wait(k):
        row = pl.ds(pl.multiple_of((half * PLANE + k) * ROWS, ROWS), ROWS)
        pltpu.make_async_remote_copy(
            wall.at[row, :], wall.at[row, :], pl_s.at[0], own_r.at[k], device_id=dev(z, y, k), device_id_type=MESH
        ).wait_recv()

    def ring_copy(b, s, k, d):
        row = pl.ds(pl.multiple_of(k * ROWS, ROWS), ROWS)
        to = lax.rem(z + jnp.where(d == 0, 1, NZ - 1), NZ) if not isinstance(d, int) else (z_up, z_dn)[d]
        if s < HOPS - 1:
            dst = rb.at[s + 1, row, cols(b)]
        else:
            base = (1 - to // 8) * PLANE * ROWS
            dst = wall.at[pl.ds(pl.multiple_of(base + k * ROWS, ROWS), ROWS), cols(b)]
        return pltpu.make_async_remote_copy(
            rb.at[s, row, cols(b)], dst, ring_s.at[0], ring_r.at[b, s, k], device_id=dev(to, y, me), device_id_type=MESH
        )

    def ring_wait(b, s, k):
        if s < HOPS - 1:
            dst = rb.at[s + 1, pl.ds(k * ROWS, ROWS), cols(b)]
        else:
            dst = wall.at[pl.ds(pl.multiple_of(far * ROWS + k * ROWS, ROWS), ROWS), cols(b)]
        pltpu.make_async_remote_copy(
            dst, dst, ring_s.at[0], ring_r.at[b, s, k], device_id=up, device_id_type=MESH
        ).wait_recv()

    def bring_copy(s, d):
        rows = pl.ds(d * 16, 16)
        src = lf.at[rows, :] if s == 0 else rbb.at[s - 1, rows, :]
        return pltpu.make_async_remote_copy(
            src, rbb.at[s, rows, :], bring_s.at[s, d], bring_r.at[s, d], device_id=(up, dn)[d], device_id_type=MESH
        )

    def bplane_copy(i, which):
        k = plane[i]
        if which == 0:
            src, q = lf, t
        else:
            src, q = rbb.at[HOPS - 1], far + me
        return pltpu.make_async_remote_copy(
            src,
            ball.at[pl.ds(pl.multiple_of(q * ROWS, ROWS), ROWS), :],
            bp_s.at[which, i],
            bp_r.at[which, me],
            device_id=dev(z, y, k),
            device_id_type=MESH,
        )

    def bplane_wait(k, which):
        q = (t // PLANE) * PLANE + k if which == 0 else far + k
        dst = ball.at[pl.ds(pl.multiple_of(q * ROWS, ROWS), ROWS), :]
        pltpu.make_async_remote_copy(
            dst, dst, bp_s.at[which, 0], bp_r.at[which, k], device_id=up, device_id_type=MESH
        ).wait_recv()

    def y_copy(b, i):
        return pltpu.make_async_remote_copy(
            psy[b].at[y], psy[b].at[y], y_s.at[b, i], y_r.at[b, y], device_id=dev(z, y_peers[i], me), device_id_type=MESH
        )

    def y_wait(b, q):
        pltpu.make_async_remote_copy(
            psy[b].at[q], psy[b].at[q], y_s.at[b, 0], y_r.at[b, q], device_id=up, device_id_type=MESH
        ).wait_recv()

    def z_copy(b, i):
        return pltpu.make_async_remote_copy(
            psz[b].at[zlo],
            psz[b].at[zlo],
            z_s.at[b, i],
            z_r.at[b, zlo],
            device_id=dev(half * 8 + z_peers[i], y, me),
            device_id_type=MESH,
        )

    def z_wait(b, q):
        pltpu.make_async_remote_copy(
            psz[b].at[q], psz[b].at[q], z_s.at[b, 0], z_r.at[b, q], device_id=up, device_id_type=MESH
        ).wait_recv()

    def squares(b, j):
        c = slice((C0[b] + j) * BLOCK, (C0[b] + j + 1) * BLOCK)
        total = jnp.zeros((1, BLOCK), jnp.float32)
        for i in range(4):
            r = slice(i * BLOCK, (i + 1) * BLOCK)
            v = wall[r, c].astype(jnp.float32) + jnp.dot(
                ball[r, :], rfv[:, c], preferred_element_type=jnp.float32
            )
            comb[r, c] = v
            total = total + jnp.sum(v * v, axis=0, keepdims=True)
        psy[b][pl.ds(y, 1), j : j + 1, :] = total[None]

    def finish(b, j):
        g = C0[b] + j
        c = slice(g * BLOCK, (g + 1) * BLOCK)
        total = jnp.sum(psz[b][:, j, :], axis=0, keepdims=True)
        factor = magv[pl.ds(t * 13 + g, 1), :] / jnp.sqrt(total + EPS)
        rid = lax.broadcasted_iota(jnp.int32, (8, BLOCK), 0)
        cid = lax.broadcasted_iota(jnp.int32, (8, BLOCK), 1)
        for i in range(4):
            r = slice(i * BLOCK, (i + 1) * BLOCK)
            m = (comb[r, c] * factor).astype(jnp.bfloat16).astype(jnp.float32)
            top = jnp.max(jnp.max(jnp.abs(m), axis=0, keepdims=True), axis=1, keepdims=True)
            outv[r, c] = (m * (1.0 / (top + EPS))).astype(jnp.bfloat16)
            scv[...] = jnp.where((rid == i) & (cid == g), top, scv[...])

    def out_copy(b):
        return pltpu.make_async_copy(outv.at[:, cols(b)], out.at[:, cols(b)], outs.at[b])

    def pieces(b):
        def arrive():
            for k in range(PLANE):
                ring_wait(b, HOPS - 1, k)
            if b == 0:
                for k in plane:
                    own_wait(k)
                    bplane_wait(k, 0)
                    bplane_wait(k, 1)
                for c in loads:
                    c.wait()

        def y_send():
            for i in range(3):
                y_copy(b, i).start()

        def y_sum():
            for q in y_peers:
                y_wait(b, q)
            psz[b][pl.ds(zlo, 1)] = jnp.sum(psy[b][...], axis=0, keepdims=True)
            for i in range(7):
                z_copy(b, i).start()

        def z_sum():
            for q in z_peers:
                z_wait(b, q)

        todo = [(6, arrive)]
        todo += [(7 + j, functools.partial(squares, b, j)) for j in range(NB[b])]
        todo += [(7 + NB[b], y_send), (12 + NB[b], y_sum), (22 + NB[b], z_sum)]
        todo += [(23 + NB[b] + j, functools.partial(finish, b, j)) for j in range(NB[b])]
        todo += [(23 + 2 * NB[b], lambda: out_copy(b).start())]
        return todo

    for d in range(2):
        bring_copy(0, d).start()
    for i in range(7):
        stage_copy(0, i).start()
    for i in range(7):
        bplane_copy(i, 0).start()
    for i in range(7):
        own_copy(i).start()
    for b in range(1, len(NB)):
        for i in range(7):
            stage_copy(b, i).start()
    scv[...] = jnp.zeros_like(scv)

    queue = []
    for b in range(len(NB)):
        slot = 0
        for s in range(HOPS):
            if b == 0 and s > 0:
                for d in range(2):
                    bring_copy(s - 1, d).wait_recv()
                    bring_copy(s, d).start()
            order = [me] + plane if s == 0 else [0, 4, 1, 5, 2, 6, 3, 7]
            for n, k in enumerate(order):
                if s == 0:
                    if b == 0 and n == 0:
                        own_stage.wait()
                    if n > 0:
                        stage_wait(b, k)
                    ring_copy(b, s, k, jnp.where(k < 4, 0, 1)).start()
                else:
                    ring_wait(b, s - 1, k)
                    ring_copy(b, s, k, k // 4).start()
                if n % 2 == 1:
                    while queue and queue[0][0] <= slot:
                        queue.pop(0)[1]()
                        break
                    slot += 1
        if b == 0:
            for d in range(2):
                bring_copy(HOPS - 1, d).wait_recv()
            fill = pltpu.make_async_copy(
                rbb.at[HOPS - 1], ball.at[pl.ds(pl.multiple_of((far + me) * ROWS, ROWS), ROWS), :], loc.at[5]
            )
            fill.start()
            loads.append(fill)
            for i in range(7):
                bplane_copy(i, 1).start()
        while queue:
            queue.pop(0)[1]()
        queue = pieces(b)
    while queue:
        queue.pop(0)[1]()

    pltpu.make_async_remote_copy(rb, rb, ring_s.at[0], ring_r.at[0, 0, 0], device_id=up, device_id_type=MESH).wait_send()
    both = wall.at[pl.ds(0, 14 * ROWS), :]
    pltpu.make_async_remote_copy(both, both, pl_s.at[0], own_r.at[0], device_id=up, device_id_type=MESH).wait_send()
    for s in range(HOPS):
        for d in range(2):
            bring_copy(s, d).wait_send()
    for i in range(7):
        for which in range(2):
            bplane_copy(i, which).wait_send()
    for b in range(len(NB)):
        for i in range(3):
            y_copy(b, i).wait_send()
        for i in range(7):
            z_copy(b, i).wait_send()
    scales[...] = scv[0:4, 0:13]
    for b in range(len(NB)):
        out_copy(b).wait()


def body(base_weight, left_factor, right_factor, magnitude):
    bf, f32 = jnp.bfloat16, jnp.float32
    dma = pltpu.SemaphoreType.DMA
    nb = len(NB)
    anywhere = pl.BlockSpec(memory_space=pl.ANY)
    return pl.pallas_call(
        kernel,
        name="merge",
        out_shape=(
            jax.ShapeDtypeStruct((16 * ROWS, COLS), bf),
            jax.ShapeDtypeStruct((4, 13), f32),
        ),
        in_specs=[anywhere] * 4,
        out_specs=(anywhere, pl.BlockSpec(memory_space=pltpu.VMEM)),
        scratch_shapes=[
            pltpu.VMEM((16 * ROWS, COLS), bf),
            pltpu.VMEM((HOPS, PLANE * ROWS, COLS), bf),
            pltpu.VMEM((16 * ROWS, 64), bf),
            pltpu.VMEM((HOPS, ROWS, 64), bf),
            pltpu.VMEM((64, COLS), bf),
            pltpu.VMEM((208, BLOCK), f32),
            pltpu.VMEM((16 * ROWS, COLS), f32),
            pltpu.VMEM((16 * ROWS, COLS), bf),
            *[pltpu.VMEM((NY, n, BLOCK), f32) for n in NB],
            *[pltpu.VMEM((8, n, BLOCK), f32) for n in NB],
            pltpu.VMEM((8, BLOCK), f32),
            dma((1,)),
            dma((nb, HOPS, PLANE)),
            dma((HOPS, 2)),
            dma((HOPS, 2)),
            dma((1,)),
            dma((nb, PLANE)),
            dma((PLANE,)),
            dma((2, 7)),
            dma((2, PLANE)),
            dma((nb, 3)),
            dma((nb, NY)),
            dma((nb, 7)),
            dma((nb, 8)),
            dma((6,)),
            dma((nb,)),
        ],
        compiler_params=pltpu.CompilerParams(collective_id=0, has_side_effects=True),
    )(base_weight, left_factor, right_factor, magnitude.reshape(208, BLOCK))


def solution(mesh):
    in_specs = (P(("fsdp", "tp"), None), P(("fsdp", "tp"), None), P(None, "tp"), P())
    out_specs = (P("fsdp", "tp"), P("fsdp", "tp"))
    return jax.shard_map(body, mesh=mesh, in_specs=in_specs, out_specs=out_specs, check_vma=False)
```

time: 683 us -> 127 us (0.19)
  the two profiles are of different devices: /device:TPU:96 before, /device:TPU:6 now
where the time goes in v1:
time: 127 us; the launch traced here: 125 us
  Pallas kernels  121 us (95%)
  local copies, waits for them, and re-layouts  3.35 us (3%)
    pallas_call x1, Pallas kernels, body(): pl.pallas_call(kernel, name='merge', out_shape=(jax.ShapeDtypeStruct((16...  121 us
    unnamed x4, local copies, waits for them, and re-layouts  3.35 us

profile of v1, /device:TPU:6, one launch (start us, length us, event | category | flops | bytes accessed | tf_op | source)
XLA Modules:
  0.0 125.0 jit_solution(16175272906361872647)
XLA Ops:
  0.6 121.0 %merge.1 = (bf16[512,1664]{1,0:T(8,128)(2,1)}, f32[4,13]{1,0:T(4,128)}) custom-call(bf16[32,26624]{1,0:T(8,128)(2,1)} %w.1, bf16[32,64]{1,0:T(8,128)(2,1)} %lf.1, bf16[64,1664]{1,0:T(8,128)(2,1)} %rf.1, f32[208,128]{1,0:T(8,128)} %bitcast.1), custom_call_target="tpu_custom_call" | custom-call | tf_op jit(solution)/shard_map/merge/pallas_call | solution.py:325
  121.6 0.0 copy-start
  121.6 2.8 %copy.8 = bf16[512,1664]{1,0:T(8,128)(2,1)} copy(bf16[512,1664]{1,0:T(8,128)(2,1)} %get-tuple-element.4) | data formatting | bytes 3407872
  124.4 0.0 copy-done
  124.4 0.6 copy.9
Async XLA Ops:
  121.6 2.8 %copy-start = (f32[4,13]{1,0:T(4,128)S(1)}, f32[4,13]{1,0:T(4,128)}, u32[]{:S(2)}) copy-start(f32[4,13]{1,0:T(4,128)} %get-tuple-element.5) | copy-start | bytes 628

commit v2 on v0

v2 whole, which is shorter than its diff:
```python
import functools

import jax
import jax.numpy as jnp
from jax import lax
from jax.experimental import pallas as pl
from jax.experimental.pallas import tpu as pltpu
from jax.sharding import PartitionSpec as P

MESH = pl.DeviceIdType.MESH
BLOCK = 128
EPS = 1e-06
NB = (5, 4, 4)
C0 = (0, 5, 9)
ROWS = 32
COLS = 1664
CHUNKS = 13
NX = 4
NY = 4
NZ = 16
HOPS = 8
PLANE = 8
UPC = 7 * BLOCK
READY = {0: 1.0, 1: 8.0, 3: 8.0, 2: 17.0}
DXS = (0, 1, 3, 2)


def ring_order():
    at = {(dx, r): [0, READY[dx]] for dx in DXS for r in range(len(NB))}
    now, order = 0.0, []
    while any(v[0] < HOPS - 1 for v in at.values()):
        ready = [(v[0], r, DXS.index(dx), dx) for (dx, r), v in at.items() if v[0] < HOPS - 1 and v[1] <= now]
        if not ready:
            now += 0.1
            continue
        s, r, _, dx = min(ready)
        order.append((now, s, dx, r))
        now += 0.18 * NB[r]
        at[dx, r] = [s + 1, now + 2.2]
    for r in range(len(NB)):
        for xs in range(NX):
            order.append((now, HOPS - 1, xs, r))
            now += 0.18 * NB[r]
    return order


def kernel(
    w, lf, rf, mag, out, scales, wall, rb, ball, rbb, rfv, apv, magv, facv, comb, outv, ps, ry, pay, zs, tz, scv,
    ring_s, ring_r, bring_s, bring_r, pl_s, st_r, own_r, bp_s, bp_r, ap_s, ap_r, ay_s, ay_r, y_s, y_r, z_s, z_r,
    g_s, g_r, loc, outs,
):
    f, t = lax.axis_index("fsdp"), lax.axis_index("tp")
    zlo, y = f // NY, lax.rem(f, NY)
    half, x, core = t // PLANE, lax.rem(t, PLANE) // 2, lax.rem(t, 2)
    z = half * 8 + zlo
    me = x * 2 + core
    far = (1 - half) * PLANE

    def dev(zz, yy, k):
        return (lax.rem(zz, 8) * NY + yy, (zz // 8) * PLANE + k)

    z_up, z_dn = lax.rem(z + 1, NZ), lax.rem(z + NZ - 1, NZ)
    up, dn = dev(z_up, y, me), dev(z_dn, y, me)
    plane = [lax.rem(x + dx, NX) * 2 + lax.rem(core + dc, 2) for dx in DXS for dc in (0, 1)][1:]
    y_peers = [lax.rem(y + d, NY) for d in range(1, NY)]
    z_peers = [lax.rem(z + d, NZ) for d in range(1, NZ)]

    def rows(k, n=ROWS):
        return pl.ds(pl.multiple_of(k * n, n), n)

    def cols(r):
        return pl.ds(C0[r] * BLOCK, NB[r] * BLOCK)

    def remote(src, dst, send, recv, to):
        return pltpu.make_async_remote_copy(src, dst, send, recv, device_id=to, device_id_type=MESH)

    own_stage = pltpu.make_async_copy(
        w.at[:, pl.ds(pl.multiple_of((far + me) * COLS, BLOCK), COLS)], rb.at[0, rows(me), :], loc.at[4]
    )
    loads = [
        pltpu.make_async_copy(rf, rfv, loc.at[0]),
        pltpu.make_async_copy(mag, magv, loc.at[1]),
        pltpu.make_async_copy(lf, ball.at[rows(t), :], loc.at[2]),
        pltpu.make_async_copy(w.at[:, pl.ds(pl.multiple_of(t * COLS, BLOCK), COLS)], wall.at[rows(t), :], loc.at[3]),
    ]
    own_stage.start()
    for c in loads:
        c.start()

    barrier = pltpu.get_barrier_semaphore()
    peers = [up, dn] + [dev(z, y, k) for k in plane] + [dev(z, q, me) for q in y_peers]
    for p in peers:
        pl.semaphore_signal(barrier, inc=1, device_id=p, device_id_type=MESH)
    pl.semaphore_wait(barrier, len(peers))

    def stage_copy(i):
        k = plane[i]
        src = w.at[:, pl.ds(pl.multiple_of((far + k) * COLS, BLOCK), COLS)]
        return remote(src, rb.at[0, rows(me), :], pl_s.at[0], st_r.at[me], dev(z, y, k))

    def stage_wait(k):
        remote(rb.at[0, rows(k), :], rb.at[0, rows(k), :], pl_s.at[0], st_r.at[k], up).wait_recv()

    def own_copy(i):
        k = plane[i]
        src = w.at[:, pl.ds(pl.multiple_of((half * PLANE + k) * COLS, BLOCK), COLS)]
        return remote(src, wall.at[rows(t), :], pl_s.at[0], own_r.at[me], dev(z, y, k))

    def own_wait(k):
        row = rows(half * PLANE + k)
        remote(wall.at[row, :], wall.at[row, :], pl_s.at[0], own_r.at[k], up).wait_recv()

    def ring_copy(r, s, k, d):
        to = (z_up, z_dn)[d] if isinstance(d, int) else lax.rem(z + jnp.where(d == 0, 1, NZ - 1), NZ)
        if s < HOPS - 1:
            dst = rb.at[s + 1, rows(k), cols(r)]
        else:
            dst = wall.at[rows((1 - to // 8) * PLANE + k), cols(r)]
        return remote(rb.at[s, rows(k), cols(r)], dst, ring_s.at[0], ring_r.at[r, s, k], dev(to, y, me))

    def ring_wait(r, s, k):
        dst = rb.at[s + 1, rows(k), cols(r)] if s < HOPS - 1 else wall.at[rows(far + k), cols(r)]
        remote(dst, dst, ring_s.at[0], ring_r.at[r, s, k], up).wait_recv()

    def bring_copy(s, d):
        part = pl.ds(d * 16, 16)
        src = lf.at[part, :] if s == 0 else rbb.at[s - 1, part, :]
        return remote(src, rbb.at[s, part, :], bring_s.at[s, d], bring_r.at[s, d], (up, dn)[d])

    def bplane_copy(i, which):
        src, q = (lf, t) if which == 0 else (rbb.at[HOPS - 1], far + me)
        return remote(src, ball.at[rows(q), :], bp_s.at[which, i], bp_r.at[which, me], dev(z, y, plane[i]))

    def bplane_wait(k, which):
        dst = ball.at[rows((half * PLANE if which == 0 else far) + k), :]
        remote(dst, dst, bp_s.at[which, 0], bp_r.at[which, k], up).wait_recv()

    def chain(d, own):
        c = (pl.ds(0, UPC), pl.ds(UPC, COLS - UPC))[d]
        dst = apv.at[rows(y, 16), c]
        return remote(rf.at[rows(y, 16), c] if own else dst, dst, ap_s.at[d], ap_r.at[d], (up, dn)[d])

    def chain_step(j):
        for d in range(2):
            place = zlo if d == 0 else 7 - zlo
            if j == 0:
                pl.when(place == 7)(lambda: chain(d, True).start())
            else:

                @pl.when(place == j - 1)
                def _():
                    chain(d, False).wait_recv()
                    if j < 8:
                        chain(d, False).start()

    def share_copy(i):
        part = apv.at[rows(y, 16), :]
        return remote(part, part, ay_s.at[i], ay_r.at[y], dev(z, y_peers[i], me))

    def share_wait(q):
        part = apv.at[rows(q, 16), :]
        remote(part, part, ay_s.at[0], ay_r.at[q], up).wait_recv()

    def hop_step(j):
        for d in range(2):
            if j > 0:
                bring_copy(j - 1, d).wait_recv()
            if j < HOPS:
                bring_copy(j, d).start()
        chain_step(j)

    def spread():
        fill = pltpu.make_async_copy(rbb.at[HOPS - 1], ball.at[rows(far + me), :], loc.at[5])
        fill.start()
        loads.append(fill)
        for i in range(7):
            bplane_copy(i, 1).start()
        for i in range(3):
            share_copy(i).start()

    def y_copy(i):
        q = y_peers[i]
        return remote(ps.at[q], ry.at[y], y_s.at[i], y_r.at[y], dev(z, q, me))

    def y_wait(q):
        remote(ry.at[q], ry.at[q], y_s.at[0], y_r.at[q], up).wait_recv()

    def z_copy(i):
        q = z_peers[i]
        src = pay.at[jnp.where(q // 8 == half, 0, 1)]
        return remote(src, zs.at[z], z_s.at[i], z_r.at[z], dev(q, y, me))

    def z_wait(q):
        remote(zs.at[q], zs.at[q], z_s.at[0], z_r.at[q], up).wait_recv()

    def g_copy(i):
        return remote(tz.at[y], tz.at[y], g_s.at[i], g_r.at[y], dev(z, y_peers[i], me))

    def g_wait(q):
        remote(tz.at[q], tz.at[q], g_s.at[0], g_r.at[q], up).wait_recv()

    def arrive():
        for k in plane:
            own_wait(k)
            bplane_wait(k, 0)
        for c in loads[:4]:
            c.wait()
        for q in y_peers:
            share_wait(q)

    mine = rows(half, 256)

    def squares(g):
        c = slice(g * BLOCK, (g + 1) * BLOCK)
        left = ball[mine, :]
        v = wall[mine, c].astype(jnp.float32) + jnp.dot(left, rfv[:, c], preferred_element_type=jnp.float32)
        comb[:, c] = v
        ps[g // 4, 0, g % 4 : g % 4 + 1, :] = jnp.sum(v * v, axis=0, keepdims=True)
        u = rb[0, :, c].astype(jnp.float32) + jnp.dot(left, apv[:, c], preferred_element_type=jnp.float32)
        ps[g // 4, 1, g % 4 : g % 4 + 1, :] = jnp.sum(u * u, axis=0, keepdims=True)

    def y_send():
        for i in range(3):
            y_copy(i).start()
        ry[pl.ds(y, 1)] = ps[pl.ds(y, 1)]

    def z_send():
        for q in y_peers:
            y_wait(q)
        pay[...] = jnp.sum(ry[...], axis=0)
        zs[pl.ds(z, 1)] = pay[0:1]
        for i in range(15):
            z_copy(i).start()

    def g_send():
        for q in z_peers:
            z_wait(q)
        tz[pl.ds(y, 1)] = jnp.sum(zs[...], axis=0, keepdims=True)
        for i in range(3):
            g_copy(i).start()

    def factors():
        for q in y_peers:
            g_wait(q)
        for g in range(CHUNKS):
            total = tz[g // 4, g % 4 : g % 4 + 1, :]
            facv[g : g + 1, :] = magv[pl.ds(t * CHUNKS + g, 1), :] / jnp.sqrt(total + EPS)

    rid = lax.broadcasted_iota(jnp.int32, (8, BLOCK), 0)
    cid = lax.broadcasted_iota(jnp.int32, (8, BLOCK), 1)

    def quantize(v, g, block_row):
        m = (v * facv[g : g + 1, :]).astype(jnp.bfloat16).astype(jnp.float32)
        top = jnp.max(jnp.max(jnp.abs(m), axis=0, keepdims=True), axis=1, keepdims=True)
        outv[rows(block_row, BLOCK), g * BLOCK : (g + 1) * BLOCK] = (m * (1.0 / (top + EPS))).astype(jnp.bfloat16)
        scv[...] = jnp.where((rid == block_row) & (cid == g), top, scv[...])

    def finish_own(g):
        for i in range(2):
            quantize(comb[i * BLOCK : (i + 1) * BLOCK, g * BLOCK : (g + 1) * BLOCK], g, half * 2 + i)

    def finish_far(g, i):
        c = slice(g * BLOCK, (g + 1) * BLOCK)
        row = rows((1 - half) * 2 + i, BLOCK)
        v = wall[row, c].astype(jnp.float32) + jnp.dot(ball[row, :], rfv[:, c], preferred_element_type=jnp.float32)
        quantize(v, g, (1 - half) * 2 + i)

    def own_out():
        return pltpu.make_async_copy(outv.at[mine, :], out.at[mine, :], outs.at[0])

    def far_out(r, i):
        row = rows((1 - half) * 2 + i, BLOCK)
        return pltpu.make_async_copy(outv.at[row, cols(r)], out.at[row, cols(r)], outs.at[1 + r * 2 + i])

    def ready_far():
        loads[4].wait()
        for k in plane:
            bplane_wait(k, 1)

    todo = [(1.5 + 3.0 * j, functools.partial(hop_step, j)) for j in range(9)]
    todo += [(26.0, spread), (30.0, arrive)]
    todo += [(30.5 + 0.7 * g, functools.partial(squares, g)) for g in range(CHUNKS)]
    todo += [(40.0, y_send), (44.0, z_send), (54.0, g_send), (57.5, factors)]
    todo += [(58.0, ready_far)]
    todo += [(58.0 + 0.6 * g, functools.partial(finish_own, g)) for g in range(CHUNKS)]
    todo += [(66.0, lambda: own_out().start())]

    own_stage.wait()
    for r in range(len(NB)):
        ring_copy(r, 0, me, core).start()
    for i in range(7):
        stage_copy(i).start()
    for i in range(7):
        bplane_copy(i, 0).start()
    for i in range(7):
        own_copy(i).start()
    ps[...] = jnp.zeros_like(ps)
    scv[...] = jnp.zeros_like(scv)

    staged = set()
    for now, s, dx, r in ring_order():
        if todo and todo[0][0] <= now:
            todo.pop(0)[1]()
        if s == 0 and dx == 0:
            k = x * 2 + 1 - core
            if dx not in staged:
                stage_wait(k)
                staged.add(dx)
            ring_copy(r, 0, k, 1 - core).start()
            continue
        for d in range(2):
            k = (dx if s == HOPS - 1 else lax.rem(x + dx, NX)) * 2 + d
            if s == 0:
                if dx not in staged:
                    stage_wait(k)
            else:
                ring_wait(r, s - 1, k)
            ring_copy(r, s, k, d).start()
        if s == 0:
            staged.add(dx)
    for _, task in todo:
        task()

    for r in range(len(NB)):
        for i in range(2):
            for k in range(4 * i, 4 * i + 4):
                ring_wait(r, HOPS - 1, k)
            for j in range(NB[r]):
                finish_far(C0[r] + j, i)
            far_out(r, i).start()

    scales[...] = scv[0:4, 0:CHUNKS]
    remote(rb, rb, ring_s.at[0], ring_r.at[0, 0, 0], up).wait_send()
    both = wall.at[pl.ds(0, 14 * ROWS), :]
    remote(both, both, pl_s.at[0], own_r.at[0], up).wait_send()
    for s in range(HOPS):
        for d in range(2):
            bring_copy(s, d).wait_send()
    for i in range(7):
        for which in range(2):
            bplane_copy(i, which).wait_send()
    for d in range(2):
        chain(d, False).wait_send()
    for i in range(3):
        share_copy(i).wait_send()
        y_copy(i).wait_send()
        g_copy(i).wait_send()
    for i in range(15):
        z_copy(i).wait_send()
    own_out().wait()
    for r in range(len(NB)):
        for i in range(2):
            far_out(r, i).wait()


def body(base_weight, left_factor, right_factor, magnitude):
    bf, f32 = jnp.bfloat16, jnp.float32
    dma = pltpu.SemaphoreType.DMA
    nb = len(NB)
    anywhere = pl.BlockSpec(memory_space=pl.ANY)
    return pl.pallas_call(
        kernel,
        name="merge",
        out_shape=(
            jax.ShapeDtypeStruct((16 * ROWS, COLS), bf),
            jax.ShapeDtypeStruct((4, CHUNKS), f32),
        ),
        in_specs=[anywhere] * 4,
        out_specs=(anywhere, pl.BlockSpec(memory_space=pltpu.VMEM)),
        scratch_shapes=[
            pltpu.VMEM((16 * ROWS, COLS), bf),
            pltpu.VMEM((HOPS, PLANE * ROWS, COLS), bf),
            pltpu.VMEM((16 * ROWS, 64), bf),
            pltpu.VMEM((HOPS, ROWS, 64), bf),
            pltpu.VMEM((64, COLS), bf),
            pltpu.VMEM((64, COLS), bf),
            pltpu.VMEM((208, BLOCK), f32),
            pltpu.VMEM((16, BLOCK), f32),
            pltpu.VMEM((8 * ROWS, COLS), f32),
            pltpu.VMEM((16 * ROWS, COLS), bf),
            pltpu.VMEM((NY, 2, 4, BLOCK), f32),
            pltpu.VMEM((NY, 2, 4, BLOCK), f32),
            pltpu.VMEM((2, 4, BLOCK), f32),
            pltpu.VMEM((NZ, 4, BLOCK), f32),
            pltpu.VMEM((NY, 4, BLOCK), f32),
            pltpu.VMEM((8, BLOCK), f32),
            dma((1,)),
            dma((nb, HOPS, PLANE)),
            dma((HOPS, 2)),
            dma((HOPS, 2)),
            dma((1,)),
            dma((PLANE,)),
            dma((PLANE,)),
            dma((2, 7)),
            dma((2, PLANE)),
            dma((2,)),
            dma((2,)),
            dma((3,)),
            dma((NY,)),
            dma((3,)),
            dma((NY,)),
            dma((15,)),
            dma((NZ,)),
            dma((3,)),
            dma((NY,)),
            dma((6,)),
            dma((1 + 2 * nb,)),
        ],
        compiler_params=pltpu.CompilerParams(collective_id=0, has_side_effects=True),
    )(base_weight, left_factor, right_factor, magnitude.reshape(208, BLOCK))


def solution(mesh):
    in_specs = (P(("fsdp", "tp"), None), P(("fsdp", "tp"), None), P(None, "tp"), P())
    out_specs = (P("fsdp", "tp"), P("fsdp", "tp"))
    return jax.shard_map(body, mesh=mesh, in_specs=in_specs, out_specs=out_specs, check_vma=False)
```

time: 683 us -> 105 us (0.15)
  the two profiles are of different devices: /device:TPU:96 before, /device:TPU:1 now
where the time goes in v2:
time: 105 us
  Pallas kernels  101 us (96%)
  local copies, waits for them, and re-layouts  3.35 us (3%)
    pallas_call x1, Pallas kernels, body(): pl.pallas_call(kernel, name='merge', out_shape=(jax.ShapeDtypeStruct((16...  101 us
    unnamed x4, local copies, waits for them, and re-layouts  3.35 us

profile of v2, /device:TPU:1, one launch (start us, length us, event | category | flops | bytes accessed | tf_op | source)
XLA Modules:
  0.0 105.3 jit_solution(4486322018763355862)
XLA Ops:
  0.6 101.3 %merge.1 = (bf16[512,1664]{1,0:T(8,128)(2,1)}, f32[4,13]{1,0:T(4,128)}) custom-call(bf16[32,26624]{1,0:T(8,128)(2,1)} %w.1, bf16[32,64]{1,0:T(8,128)(2,1)} %lf.1, bf16[64,1664]{1,0:T(8,128)(2,1)} %rf.1, f32[208,128]{1,0:T(8,128)} %bitcast.1), custom_call_target="tpu_custom_call" | custom-call | tf_op jit(solution)/shard_map/merge/pallas_call | solution.py:361
  101.9 0.0 copy-start
  101.9 2.8 %copy.8 = bf16[512,1664]{1,0:T(8,128)(2,1)} copy(bf16[512,1664]{1,0:T(8,128)(2,1)} %get-tuple-element.4) | data formatting | bytes 3407872
  104.7 0.0 copy-done
  104.7 0.6 copy.9
Async XLA Ops:
  101.9 2.8 %copy-start = (f32[4,13]{1,0:T(4,128)S(1)}, f32[4,13]{1,0:T(4,128)}, u32[]{:S(2)}) copy-start(f32[4,13]{1,0:T(4,128)} %get-tuple-element.5) | copy-start | bytes 628

commit v3 on v2

--- a/solution.py
+++ b/solution.py
@@ -21,7 +21,7 @@
 HOPS = 8
 PLANE = 8
 UPC = 7 * BLOCK
-READY = {0: 1.0, 1: 8.0, 3: 8.0, 2: 17.0}
+READY = {0: 1.0, 1: 12.0, 3: 12.0, 2: 36.0}
 DXS = (0, 1, 3, 2)
 
 
@@ -45,9 +45,9 @@
 
 
 def kernel(
-    w, lf, rf, mag, out, scales, wall, rb, ball, rbb, rfv, apv, magv, facv, comb, outv, ps, ry, pay, zs, tz, scv,
+    w, lf, rf, mag, outv, scales, wall, rb, ball, rbb, rfv, apv, magv, facv, comb, ps, ry, pay, zs, tz, scv,
     ring_s, ring_r, bring_s, bring_r, pl_s, st_r, own_r, bp_s, bp_r, ap_s, ap_r, ay_s, ay_r, y_s, y_r, z_s, z_r,
-    g_s, g_r, loc, outs,
+    g_s, g_r, loc,
 ):
     f, t = lax.axis_index("fsdp"), lax.axis_index("tp")
     zlo, y = f // NY, lax.rem(f, NY)
@@ -199,7 +199,20 @@
     def g_wait(q):
         remote(tz.at[q], tz.at[q], g_s.at[0], g_r.at[q], up).wait_recv()
 
+    staged = set()
+
+    def staged_by(dx):
+        if dx not in staged:
+            staged.add(dx)
+            for d in range(2):
+                if dx > 0:
+                    stage_wait(lax.rem(x + dx, NX) * 2 + d)
+            if dx == 0:
+                stage_wait(x * 2 + 1 - core)
+
     def arrive():
+        for dx in DXS:
+            staged_by(dx)
         for k in plane:
             own_wait(k)
             bplane_wait(k, 0)
@@ -265,13 +278,6 @@
         v = wall[row, c].astype(jnp.float32) + jnp.dot(ball[row, :], rfv[:, c], preferred_element_type=jnp.float32)
         quantize(v, g, (1 - half) * 2 + i)
 
-    def own_out():
-        return pltpu.make_async_copy(outv.at[mine, :], out.at[mine, :], outs.at[0])
-
-    def far_out(r, i):
-        row = rows((1 - half) * 2 + i, BLOCK)
-        return pltpu.make_async_copy(outv.at[row, cols(r)], out.at[row, cols(r)], outs.at[1 + r * 2 + i])
-
     def ready_far():
         loads[4].wait()
         for k in plane:
@@ -280,10 +286,9 @@
     todo = [(1.5 + 3.0 * j, functools.partial(hop_step, j)) for j in range(9)]
     todo += [(26.0, spread), (30.0, arrive)]
     todo += [(30.5 + 0.7 * g, functools.partial(squares, g)) for g in range(CHUNKS)]
-    todo += [(40.0, y_send), (44.0, z_send), (54.0, g_send), (57.5, factors)]
-    todo += [(58.0, ready_far)]
-    todo += [(58.0 + 0.6 * g, functools.partial(finish_own, g)) for g in range(CHUNKS)]
-    todo += [(66.0, lambda: own_out().start())]
+    todo += [(40.0, y_send), (44.0, z_send), (56.0, g_send), (59.5, factors)]
+    todo += [(60.0, ready_far)]
+    todo += [(60.0 + 0.6 * g, functools.partial(finish_own, g)) for g in range(CHUNKS)]
 
     own_stage.wait()
     for r in range(len(NB)):
@@ -297,27 +302,19 @@
     ps[...] = jnp.zeros_like(ps)
     scv[...] = jnp.zeros_like(scv)
 
-    staged = set()
     for now, s, dx, r in ring_order():
         if todo and todo[0][0] <= now:
             todo.pop(0)[1]()
+        if s == 0:
+            staged_by(dx)
         if s == 0 and dx == 0:
-            k = x * 2 + 1 - core
-            if dx not in staged:
-                stage_wait(k)
-                staged.add(dx)
-            ring_copy(r, 0, k, 1 - core).start()
+            ring_copy(r, 0, x * 2 + 1 - core, 1 - core).start()
             continue
         for d in range(2):
             k = (dx if s == HOPS - 1 else lax.rem(x + dx, NX)) * 2 + d
-            if s == 0:
-                if dx not in staged:
-                    stage_wait(k)
-            else:
+            if s > 0:
                 ring_wait(r, s - 1, k)
             ring_copy(r, s, k, d).start()
-        if s == 0:
-            staged.add(dx)
     for _, task in todo:
         task()
 
@@ -327,7 +324,6 @@
                 ring_wait(r, HOPS - 1, k)
             for j in range(NB[r]):
                 finish_far(C0[r] + j, i)
-            far_out(r, i).start()
 
     scales[...] = scv[0:4, 0:CHUNKS]
     remote(rb, rb, ring_s.at[0], ring_r.at[0, 0, 0], up).wait_send()
@@ -347,10 +343,6 @@
         g_copy(i).wait_send()
     for i in range(15):
         z_copy(i).wait_send()
-    own_out().wait()
-    for r in range(len(NB)):
-        for i in range(2):
-            far_out(r, i).wait()
 
 
 def body(base_weight, left_factor, right_factor, magnitude):
@@ -362,11 +354,11 @@
         kernel,
         name="merge",
         out_shape=(
-            jax.ShapeDtypeStruct((16 * ROWS, COLS), bf),
-            jax.ShapeDtypeStruct((4, CHUNKS), f32),
+            pltpu.VMEM((16 * ROWS, COLS), bf),
+            pltpu.VMEM((4, CHUNKS), f32),
         ),
         in_specs=[anywhere] * 4,
-        out_specs=(anywhere, pl.BlockSpec(memory_space=pltpu.VMEM)),
+        out_specs=(pl.BlockSpec(memory_space=pltpu.VMEM),) * 2,
         scratch_shapes=[
             pltpu.VMEM((16 * ROWS, COLS), bf),
             pltpu.VMEM((HOPS, PLANE * ROWS, COLS), bf),
@@ -377,7 +369,6 @@
             pltpu.VMEM((208, BLOCK), f32),
             pltpu.VMEM((16, BLOCK), f32),
             pltpu.VMEM((8 * ROWS, COLS), f32),
-            pltpu.VMEM((16 * ROWS, COLS), bf),
             pltpu.VMEM((NY, 2, 4, BLOCK), f32),
             pltpu.VMEM((NY, 2, 4, BLOCK), f32),
             pltpu.VMEM((2, 4, BLOCK), f32),
@@ -404,7 +395,6 @@
             dma((3,)),
             dma((NY,)),
             dma((6,)),
-            dma((1 + 2 * nb,)),
         ],
         compiler_params=pltpu.CompilerParams(collective_id=0, has_side_effects=True),
     )(base_weight, left_factor, right_factor, magnitude.reshape(208, BLOCK))

time: 105 us -> 99.3 us (0.946)
  the two profiles are of different devices: /device:TPU:1 before, /device:TPU:6 now
where the time goes in v3:
time: 99.3 us; the launch traced here: 99.2 us
  Pallas kernels  96.8 us (97%)
  local copies, waits for them, and re-layouts  1.77 us (2%)
    pallas_call x1, Pallas kernels, body(): pl.pallas_call(kernel, name='merge', out_shape=(pltpu.VMEM((16 * ROWS, CO...  96.8 us

profile of v3, /device:TPU:6, one launch (start us, length us, event | category | flops | bytes accessed | tf_op | source)
XLA Modules:
  0.0 99.2 jit_solution(6094382480991689941)
XLA Ops:
  0.6 96.8 %merge.1 = (bf16[512,1664]{1,0:T(8,128)(2,1)S(1)}, f32[4,13]{1,0:T(4,128)S(1)}) custom-call(bf16[32,26624]{1,0:T(8,128)(2,1)} %w.1, bf16[32,64]{1,0:T(8,128)(2,1)} %lf.1, bf16[64,1664]{1,0:T(8,128)(2,1)} %rf.1, f32[208,128]{1,0:T(8,128)} %bitcast.1), custom_call_target="tpu_custom_call" | custom-call | tf_op jit(solution)/shard_map/merge/pallas_call | solution.py:353
  97.4 1.2 %copy.8 = bf16[512,1664]{1,0:T(8,128)(2,1)} copy(bf16[512,1664]{1,0:T(8,128)(2,1)S(1)} %get-tuple-element.2) | data formatting | bytes 3407872
  98.6 0.6 copy.9

commit v4 on v3

--- a/solution.py
+++ b/solution.py
@@ -10,8 +10,8 @@
 MESH = pl.DeviceIdType.MESH
 BLOCK = 128
 EPS = 1e-06
-NB = (5, 4, 4)
-C0 = (0, 5, 9)
+NB = (3, 7, 3)
+C0 = (0, 3, 10)
 ROWS = 32
 COLS = 1664
 CHUNKS = 13
@@ -21,23 +21,27 @@
 HOPS = 8
 PLANE = 8
 UPC = 7 * BLOCK
-READY = {0: 1.0, 1: 12.0, 3: 12.0, 2: 36.0}
+READY = {0: 1.0, 1: 12.0, 3: 12.0, 2: 26.0}
 DXS = (0, 1, 3, 2)
 
 
 def ring_order():
-    at = {(dx, r): [0, READY[dx]] for dx in DXS for r in range(len(NB))}
+    at = {(dx, r): [0, READY[dx] if r else 0.0] for dx in DXS for r in range(len(NB))}
+
+    def more(r, s):
+        return s < HOPS - (1 if r else 0)
+
     now, order = 0.0, []
-    while any(v[0] < HOPS - 1 for v in at.values()):
-        ready = [(v[0], r, DXS.index(dx), dx) for (dx, r), v in at.items() if v[0] < HOPS - 1 and v[1] <= now]
+    while any(more(r, v[0]) for (_, r), v in at.items()):
+        ready = [(min(r, 1), v[0], r, DXS.index(dx), dx) for (dx, r), v in at.items() if more(r, v[0]) and v[1] <= now]
         if not ready:
             now += 0.1
             continue
-        s, r, _, dx = min(ready)
+        _, s, r, _, dx = min(ready)
         order.append((now, s, dx, r))
         now += 0.18 * NB[r]
         at[dx, r] = [s + 1, now + 2.2]
-    for r in range(len(NB)):
+    for r in range(1, len(NB)):
         for xs in range(NX):
             order.append((now, HOPS - 1, xs, r))
             now += 0.18 * NB[r]
@@ -47,7 +51,7 @@
 def kernel(
     w, lf, rf, mag, outv, scales, wall, rb, ball, rbb, rfv, apv, magv, facv, comb, ps, ry, pay, zs, tz, scv,
     ring_s, ring_r, bring_s, bring_r, pl_s, st_r, own_r, bp_s, bp_r, ap_s, ap_r, ay_s, ay_r, y_s, y_r, z_s, z_r,
-    g_s, g_r, loc,
+    g_s, g_r, sc_s, sc_r, loc,
 ):
     f, t = lax.axis_index("fsdp"), lax.axis_index("tp")
     zlo, y = f // NY, lax.rem(f, NY)
@@ -68,6 +72,11 @@
     def rows(k, n=ROWS):
         return pl.ds(pl.multiple_of(k * n, n), n)
 
+    rest = pl.ds(C0[1] * BLOCK, COLS - C0[1] * BLOCK)
+
+    def wide(k):
+        return pl.ds(pl.multiple_of((far + k) * COLS + C0[1] * BLOCK, BLOCK), COLS - C0[1] * BLOCK)
+
     def cols(r):
         return pl.ds(C0[r] * BLOCK, NB[r] * BLOCK)
 
@@ -75,7 +84,7 @@
         return pltpu.make_async_remote_copy(src, dst, send, recv, device_id=to, device_id_type=MESH)
 
     own_stage = pltpu.make_async_copy(
-        w.at[:, pl.ds(pl.multiple_of((far + me) * COLS, BLOCK), COLS)], rb.at[0, rows(me), :], loc.at[4]
+        w.at[:, wide(me)], rb.at[0, rows(me), rest], loc.at[4]
     )
     loads = [
         pltpu.make_async_copy(rf, rfv, loc.at[0]),
@@ -95,32 +104,54 @@
 
     def stage_copy(i):
         k = plane[i]
-        src = w.at[:, pl.ds(pl.multiple_of((far + k) * COLS, BLOCK), COLS)]
-        return remote(src, rb.at[0, rows(me), :], pl_s.at[0], st_r.at[me], dev(z, y, k))
+        return remote(w.at[:, wide(k)], rb.at[0, rows(me), rest], pl_s.at[0], st_r.at[me], dev(z, y, k))
 
     def stage_wait(k):
-        remote(rb.at[0, rows(k), :], rb.at[0, rows(k), :], pl_s.at[0], st_r.at[k], up).wait_recv()
+        remote(rb.at[0, rows(k), rest], rb.at[0, rows(k), rest], pl_s.at[0], st_r.at[k], up).wait_recv()
 
     def own_copy(i):
         k = plane[i]
         src = w.at[:, pl.ds(pl.multiple_of((half * PLANE + k) * COLS, BLOCK), COLS)]
-        return remote(src, wall.at[rows(t), :], pl_s.at[0], own_r.at[me], dev(z, y, k))
+        return remote(src, wall.at[rows(t), :], pl_s.at[1], own_r.at[me], dev(z, y, k))
 
     def own_wait(k):
         row = rows(half * PLANE + k)
-        remote(wall.at[row, :], wall.at[row, :], pl_s.at[0], own_r.at[k], up).wait_recv()
+        remote(wall.at[row, :], wall.at[row, :], pl_s.at[1], own_r.at[k], up).wait_recv()
 
     def ring_copy(r, s, k, d):
         to = (z_up, z_dn)[d] if isinstance(d, int) else lax.rem(z + jnp.where(d == 0, 1, NZ - 1), NZ)
-        if s < HOPS - 1:
-            dst = rb.at[s + 1, rows(k), cols(r)]
+        if s < HOPS - 1 or r == 0:
+            dst = rb.at[(s + 1) % HOPS, rows(k), cols(r)]
         else:
             dst = wall.at[rows((1 - to // 8) * PLANE + k), cols(r)]
-        return remote(rb.at[s, rows(k), cols(r)], dst, ring_s.at[0], ring_r.at[r, s, k], dev(to, y, me))
+        src = rb.at[s, rows(k), cols(r)]
+        if s == 0 and r == 0:
+            src = w.at[:, pl.ds(pl.multiple_of((far + k) * COLS, BLOCK), NB[0] * BLOCK)]
+        return remote(src, dst, ring_s.at[0], ring_r.at[r, s, k], dev(to, y, me))
 
     def ring_wait(r, s, k):
-        dst = rb.at[s + 1, rows(k), cols(r)] if s < HOPS - 1 else wall.at[rows(far + k), cols(r)]
+        if s < HOPS - 1 or r == 0:
+            dst = rb.at[(s + 1) % HOPS, rows(k), cols(r)]
+        else:
+            dst = wall.at[rows(far + k), cols(r)]
         remote(dst, dst, ring_s.at[0], ring_r.at[r, s, k], up).wait_recv()
+
+    def scatter_copy(i):
+        src = rb.at[0, rows(plane[i]), cols(0)]
+        return remote(src, wall.at[rows(far + me), cols(0)], sc_s.at[i], sc_r.at[me], dev(z, y, plane[i]))
+
+    def scatter_wait(k):
+        dst = wall.at[rows(far + k), cols(0)]
+        remote(dst, dst, sc_s.at[0], sc_r.at[k], up).wait_recv()
+
+    keep = pltpu.make_async_copy(rb.at[0, rows(me), cols(0)], wall.at[rows(far + me), cols(0)], loc.at[6])
+
+    def scatter():
+        for k in range(PLANE):
+            ring_wait(0, HOPS - 1, k)
+        for i in range(7):
+            scatter_copy(i).start()
+        keep.start()
 
     def bring_copy(s, d):
         part = pl.ds(d * 16, 16)
@@ -223,12 +254,21 @@
 
     mine = rows(half, 256)
 
+    def far_values(g, row):
+        c = slice(g * BLOCK, (g + 1) * BLOCK)
+        return wall[row, c].astype(jnp.float32) + jnp.dot(ball[row, :], rfv[:, c], preferred_element_type=jnp.float32)
+
     def squares(g):
         c = slice(g * BLOCK, (g + 1) * BLOCK)
         left = ball[mine, :]
         v = wall[mine, c].astype(jnp.float32) + jnp.dot(left, rfv[:, c], preferred_element_type=jnp.float32)
         comb[:, c] = v
-        ps[g // 4, 0, g % 4 : g % 4 + 1, :] = jnp.sum(v * v, axis=0, keepdims=True)
+        total = jnp.sum(v * v, axis=0, keepdims=True)
+        if g < NB[0]:
+            u = far_values(g, rows(1 - half, 256))
+            ps[g // 4, 0, g % 4 : g % 4 + 1, :] = total + jnp.sum(u * u, axis=0, keepdims=True)
+            return
+        ps[g // 4, 0, g % 4 : g % 4 + 1, :] = total
         u = rb[0, :, c].astype(jnp.float32) + jnp.dot(left, apv[:, c], preferred_element_type=jnp.float32)
         ps[g // 4, 1, g % 4 : g % 4 + 1, :] = jnp.sum(u * u, axis=0, keepdims=True)
 
@@ -271,27 +311,41 @@
     def finish_own(g):
         for i in range(2):
             quantize(comb[i * BLOCK : (i + 1) * BLOCK, g * BLOCK : (g + 1) * BLOCK], g, half * 2 + i)
+        far_product(g)
 
     def finish_far(g, i):
+        row = rows((1 - half) * 2 + i, BLOCK)
         c = slice(g * BLOCK, (g + 1) * BLOCK)
-        row = rows((1 - half) * 2 + i, BLOCK)
-        v = wall[row, c].astype(jnp.float32) + jnp.dot(ball[row, :], rfv[:, c], preferred_element_type=jnp.float32)
-        quantize(v, g, (1 - half) * 2 + i)
+        quantize(wall[row, c].astype(jnp.float32) + comb[i * BLOCK : (i + 1) * BLOCK, c], g, (1 - half) * 2 + i)
+
+    def far_product(g):
+        c = slice(g * BLOCK, (g + 1) * BLOCK)
+        comb[:, c] = jnp.dot(ball[rows(1 - half, 256), :], rfv[:, c], preferred_element_type=jnp.float32)
 
     def ready_far():
         loads[4].wait()
         for k in plane:
             bplane_wait(k, 1)
-
-    todo = [(1.5 + 3.0 * j, functools.partial(hop_step, j)) for j in range(9)]
-    todo += [(26.0, spread), (30.0, arrive)]
-    todo += [(30.5 + 0.7 * g, functools.partial(squares, g)) for g in range(CHUNKS)]
-    todo += [(40.0, y_send), (44.0, z_send), (56.0, g_send), (59.5, factors)]
-    todo += [(60.0, ready_far)]
-    todo += [(60.0 + 0.6 * g, functools.partial(finish_own, g)) for g in range(CHUNKS)]
-
+            scatter_wait(k)
+        keep.wait()
+
+    order = ring_order()
+    landed = max(e[0] for e in order if e[3] == 0) + 3.5
+    todo = [(2.0 + 3.4 * j, functools.partial(hop_step, j)) for j in range(9)]
+    todo += [(30.0, spread), (min(landed, 32.0), scatter), (33.0, arrive)]
+    todo += [(33.5 + 0.7 * i, functools.partial(squares, NB[0] + i)) for i in range(CHUNKS - NB[0])]
+    todo += [(40.7, ready_far)]
+    todo += [(41.0 + 0.7 * i, functools.partial(squares, i)) for i in range(NB[0])]
+    todo += [(44.0, y_send), (47.5, z_send), (58.0, g_send), (61.5, factors)]
+    todo += [(62.0 + 0.4 * g, functools.partial(finish_own, g)) for g in range(CHUNKS)]
+    todo += [(67.5 + 0.4 * g, functools.partial(finish_far, g, i)) for g in range(NB[0]) for i in range(2)]
+    todo.sort(key=lambda e: e[0])
+
+    for dx in DXS:
+        for d in range(2):
+            ring_copy(0, 0, lax.rem(x + dx, NX) * 2 + d, d).start()
     own_stage.wait()
-    for r in range(len(NB)):
+    for r in range(1, len(NB)):
         ring_copy(r, 0, me, core).start()
     for i in range(7):
         stage_copy(i).start()
@@ -302,23 +356,25 @@
     ps[...] = jnp.zeros_like(ps)
     scv[...] = jnp.zeros_like(scv)
 
-    for now, s, dx, r in ring_order():
+    for now, s, dx, r in order:
         if todo and todo[0][0] <= now:
             todo.pop(0)[1]()
+        if s == 0 and r == 0:
+            continue
         if s == 0:
             staged_by(dx)
         if s == 0 and dx == 0:
             ring_copy(r, 0, x * 2 + 1 - core, 1 - core).start()
             continue
         for d in range(2):
-            k = (dx if s == HOPS - 1 else lax.rem(x + dx, NX)) * 2 + d
+            k = (dx if s == HOPS - 1 and r > 0 else lax.rem(x + dx, NX)) * 2 + d
             if s > 0:
                 ring_wait(r, s - 1, k)
             ring_copy(r, s, k, d).start()
     for _, task in todo:
         task()
 
-    for r in range(len(NB)):
+    for r in range(1, len(NB)):
         for i in range(2):
             for k in range(4 * i, 4 * i + 4):
                 ring_wait(r, HOPS - 1, k)
@@ -327,12 +383,13 @@
 
     scales[...] = scv[0:4, 0:CHUNKS]
     remote(rb, rb, ring_s.at[0], ring_r.at[0, 0, 0], up).wait_send()
-    both = wall.at[pl.ds(0, 14 * ROWS), :]
-    remote(both, both, pl_s.at[0], own_r.at[0], up).wait_send()
+    for n, part in enumerate((wall.at[pl.ds(0, 7 * ROWS), rest], wall.at[pl.ds(0, 7 * ROWS), :])):
+        remote(part, part, pl_s.at[n], own_r.at[0], up).wait_send()
     for s in range(HOPS):
         for d in range(2):
             bring_copy(s, d).wait_send()
     for i in range(7):
+        scatter_copy(i).wait_send()
         for which in range(2):
             bplane_copy(i, which).wait_send()
     for d in range(2):
@@ -345,12 +402,23 @@
         z_copy(i).wait_send()
 
 
+def put(result, scales, out, out_scales, sems):
+    copies = [pltpu.make_async_copy(scales, out_scales, sems.at[4])]
+    for i in range(4):
+        part = pl.ds(i * BLOCK, BLOCK)
+        copies.append(pltpu.make_async_copy(result.at[part, :], out.at[part, :], sems.at[i]))
+    for c in copies:
+        c.start()
+    for c in copies:
+        c.wait()
+
+
 def body(base_weight, left_factor, right_factor, magnitude):
     bf, f32 = jnp.bfloat16, jnp.float32
     dma = pltpu.SemaphoreType.DMA
     nb = len(NB)
     anywhere = pl.BlockSpec(memory_space=pl.ANY)
-    return pl.pallas_call(
+    result, scales = pl.pallas_call(
         kernel,
         name="merge",
         out_shape=(
@@ -379,7 +447,7 @@
             dma((nb, HOPS, PLANE)),
             dma((HOPS, 2)),
             dma((HOPS, 2)),
-            dma((1,)),
+            dma((2,)),
             dma((PLANE,)),
             dma((PLANE,)),
             dma((2, 7)),
@@ -394,10 +462,23 @@
             dma((NZ,)),
             dma((3,)),
             dma((NY,)),
-            dma((6,)),
+            dma((7,)),
+            dma((PLANE,)),
+            dma((7,)),
         ],
         compiler_params=pltpu.CompilerParams(collective_id=0, has_side_effects=True),
     )(base_weight, left_factor, right_factor, magnitude.reshape(208, BLOCK))
+    return pl.pallas_call(
+        put,
+        name="put",
+        out_shape=(
+            jax.ShapeDtypeStruct((16 * ROWS, COLS), bf),
+            jax.ShapeDtypeStruct((4, CHUNKS), f32),
+        ),
+        in_specs=[pl.BlockSpec(memory_space=pltpu.VMEM)] * 2,
+        out_specs=(anywhere, anywhere),
+        scratch_shapes=[dma((5,))],
+    )(*(pltpu.with_memory_space_constraint(v, pltpu.VMEM) for v in (result, scales)))
 
 
 def solution(mesh):

time: 99.3 us -> 96.6 us (0.973)
  local copies, waits for them, and re-layouts: 1.77 us -> 0 us
  Pallas kernels: 96.8 us -> 95.3 us
    pallas_call x1, Pallas kernels: 96.8 us -> 94.1 us  [body(): pl.pallas_call(kernel, name='merge', out_shape=(pltpu.VMEM((16 * ROWS, CO...]
    unnamed x2 -> x0, local copies, waits for them, and re-layouts: 1.77 us -> none
    pallas_call x0 -> x1, Pallas kernels: none -> 1.23 us  [body(): pl.pallas_call(put, name='put', out_shape=(jax.ShapeDtypeStruct((16 * ROW...]
where the time goes in v4:
time: 96.6 us; the launch traced here: 96 us
  Pallas kernels  95.3 us (99%)
    pallas_call x1, Pallas kernels, body(): pl.pallas_call(kernel, name='merge', out_shape=(pltpu.VMEM((16 * ROWS, CO...  94.1 us

profile of v4, /device:TPU:6, one launch (start us, length us, event | category | flops | bytes accessed | tf_op | source)
XLA Modules:
  0.0 96.0 jit_solution(16251028446338678957)
XLA Ops:
  0.6 94.1 %merge.1 = (bf16[512,1664]{1,0:T(8,128)(2,1)S(1)}, f32[4,13]{1,0:T(4,128)S(1)}) custom-call(bf16[32,26624]{1,0:T(8,128)(2,1)} %w.1, bf16[32,64]{1,0:T(8,128)(2,1)} %lf.1, bf16[64,1664]{1,0:T(8,128)(2,1)} %rf.1, f32[208,128]{1,0:T(8,128)} %bitcast.1), custom_call_target="tpu_custom_call" | custom-call | tf_op jit(solution)/shard_map/merge/pallas_call | solution.py:421
  94.7 1.2 %put.1 = (bf16[512,1664]{1,0:T(8,128)(2,1)}, f32[4,13]{1,0:T(4,128)}) custom-call(bf16[512,1664]{1,0:T(8,128)(2,1)S(1)} %get-tuple-element.4.result, f32[4,13]{1,0:T(4,128)S(1)} %get-tuple-element.5.scales), custom_call_target="tpu_custom_call" | custom-call | tf_op jit(solution)/shard_map/put/pallas_call | solution.py:471

commit v5 on v4

--- a/solution.py
+++ b/solution.py
@@ -10,8 +10,8 @@
 MESH = pl.DeviceIdType.MESH
 BLOCK = 128
 EPS = 1e-06
-NB = (3, 7, 3)
-C0 = (0, 3, 10)
+NB = (3, 8, 2)
+C0 = (0, 3, 11)
 ROWS = 32
 COLS = 1664
 CHUNKS = 13
@@ -331,14 +331,14 @@
 
     order = ring_order()
     landed = max(e[0] for e in order if e[3] == 0) + 3.5
-    todo = [(2.0 + 3.4 * j, functools.partial(hop_step, j)) for j in range(9)]
-    todo += [(30.0, spread), (min(landed, 32.0), scatter), (33.0, arrive)]
-    todo += [(33.5 + 0.7 * i, functools.partial(squares, NB[0] + i)) for i in range(CHUNKS - NB[0])]
-    todo += [(40.7, ready_far)]
-    todo += [(41.0 + 0.7 * i, functools.partial(squares, i)) for i in range(NB[0])]
-    todo += [(44.0, y_send), (47.5, z_send), (58.0, g_send), (61.5, factors)]
-    todo += [(62.0 + 0.4 * g, functools.partial(finish_own, g)) for g in range(CHUNKS)]
-    todo += [(67.5 + 0.4 * g, functools.partial(finish_far, g, i)) for g in range(NB[0]) for i in range(2)]
+    todo = [(2.0 + 3.2 * j, functools.partial(hop_step, j)) for j in range(9)]
+    todo += [(28.3, spread), (min(landed, 31.0), scatter), (31.0, arrive)]
+    todo += [(31.3 + 0.6 * i, functools.partial(squares, NB[0] + i)) for i in range(CHUNKS - NB[0])]
+    todo += [(37.6, ready_far)]
+    todo += [(37.8 + 0.6 * i, functools.partial(squares, i)) for i in range(NB[0])]
+    todo += [(39.8, y_send), (43.0, z_send), (54.0, g_send), (57.5, factors)]
+    todo += [(58.0 + 0.5 * g, functools.partial(finish_own, g)) for g in range(CHUNKS)]
+    todo += [(64.8 + 0.4 * g, functools.partial(finish_far, g, i)) for g in range(NB[0]) for i in range(2)]
     todo.sort(key=lambda e: e[0])
 
     for dx in DXS:

time: 96.6 us -> 96.8 us (level)
  no operation moved by 1% of the time
where the time goes in v5:
time: 96.8 us; the launch traced here: 96.7 us
  Pallas kernels  96.1 us (99%)
    pallas_call x1, Pallas kernels, body(): pl.pallas_call(kernel, name='merge', out_shape=(pltpu.VMEM((16 * ROWS, CO...  94.9 us

profile of v5, /device:TPU:6, one launch (start us, length us, event | category | flops | bytes accessed | tf_op | source)
XLA Modules:
  0.0 96.7 jit_solution(13644699270362512024)
XLA Ops:
  0.6 94.9 %merge.1 = (bf16[512,1664]{1,0:T(8,128)(2,1)S(1)}, f32[4,13]{1,0:T(4,128)S(1)}) custom-call(bf16[32,26624]{1,0:T(8,128)(2,1)} %w.1, bf16[32,64]{1,0:T(8,128)(2,1)} %lf.1, bf16[64,1664]{1,0:T(8,128)(2,1)} %rf.1, f32[208,128]{1,0:T(8,128)} %bitcast.1), custom_call_target="tpu_custom_call" | custom-call | tf_op jit(solution)/shard_map/merge/pallas_call | solution.py:421
  95.5 1.2 %put.1 = (bf16[512,1664]{1,0:T(8,128)(2,1)}, f32[4,13]{1,0:T(4,128)}) custom-call(bf16[512,1664]{1,0:T(8,128)(2,1)S(1)} %get-tuple-element.4.result, f32[4,13]{1,0:T(4,128)S(1)} %get-tuple-element.5.scales), custom_call_target="tpu_custom_call" | custom-call | tf_op jit(solution)/shard_map/put/pallas_call | solution.py:471
